TPU v7x, 128 devices: a whole 4x4x4 slice. The times are simulated.
128 devices in a mesh: seq: 128 (over y, x, z, core).
Axes of the slice: x: 4, y: 4, z: 4, core: 2. Of those that a mesh axis runs over, the one named last changes fastest.
Arguments:
- features: float32 [65536, 512], P('seq'), may hold values from -24 to 24
- preacts: float32 [3, 65536, 512], P(None, 'seq'), may hold values from -6 to 6
- teacher: float32 [3, 65536, 512], P(None, 'seq'), may hold values from -6 to 6
- cotangent: float32 [65536, 512], P('seq'), may hold values from -6 to 6
- kernels: float32 [3, 3, 512, 512], replicated, may hold values from -0.15625 to 0.15625
Outputs:
- input_grad: float32 [65536, 512], P('seq')
- kernel_grad: float32 [3, 3, 512, 512], P(None, None, 'seq')
All inputs are finite; a program needn't handle non-finite values.
Results may differ from a plain program's by a relative error of at most 0.0001.
Values sent between devices are 32-bit elements; how exact they have to be, the bound alone decides.
A program may use at most 128 MiB of HBM per device.

v0:
```python
import math

import jax
import jax.numpy as jnp
from jax import lax
from jax.experimental import pallas as pl
from jax.experimental.pallas import tpu as pltpu
from jax.sharding import PartitionSpec as P

LAYERS = 3
TAPS = 3
SIDE = 4
ROWS = 512
C = 512
CHUNKS = 4
CHUNK = ROWS // CHUNKS
STRIP = 32
SCALE = 1.0 / math.sqrt(65536)
MIMIC = 0.5
MESH = pl.DeviceIdType.MESH
F32 = jnp.float32


def cdf_of(u):
    return 0.5 * (1.0 + lax.erf(u * (1.0 / math.sqrt(2.0))))


def density_of(u):
    return jnp.exp(-0.5 * u * u) * (1.0 / math.sqrt(2.0 * math.pi))


def dot(left, right, over):
    return lax.dot_general(
        left, right, (((over,), (over,)), ((), ())), precision=lax.Precision.HIGH, preferred_element_type=F32
    )


def kernel(
    feat, pre, tea, cot, ker, out, kgrad,
    xs, pb, tb, g, gu, rb, w, kg, pbuf, r1, t1, r2, u, r3, v, r4,
    ld, ldt, ldw, ss, rs, ps, pr, s1, q1, s2, q2, s3, q3, s4, q4,
):
    me = lax.axis_index("seq")
    core = me % 2
    z = (me // 2) % SIDE
    x = (me // 8) % SIDE
    y = me // 32
    last = 127

    def device(yy, xx, zz):
        return ((yy * SIDE + xx) * SIDE + zz) * 2 + core

    mate = me + 1 - 2 * core
    across = device(y, x, (z + 2) % SIDE)
    low = z < 2
    forward = jnp.where(low, me + 8, me - 8)
    source = jnp.where(low, me - 8, me + 8)
    xp = [device(y, (x + j) % SIDE, z) for j in range(1, SIDE)]
    yp = [device((y + j) % SIDE, x, z) for j in range(1, SIDE)]
    zp = [device(y, x, (z + j) % SIDE) for j in range(1, SIDE)]

    barrier = pltpu.get_barrier_semaphore()
    always = [mate, across, *xp, *yp, *zp]
    for other in always:
        pl.semaphore_signal(barrier, inc=1, device_id=(other,), device_id_type=MESH)
    greeted = len(always)
    for step in (1, 2, 8):
        for by in (step, -step):
            there = jnp.logical_and(me + by >= 0, me + by <= last)

            @pl.when(there)
            def _():
                pl.semaphore_signal(barrier, inc=1, device_id=(me + by,), device_id_type=MESH)

            greeted = greeted + jnp.where(there, 1, 0)

    def rows(c):
        return pl.ds(c * CHUNK, CHUNK)

    loads = []
    for c in range(CHUNKS):
        r = rows(c)
        pairs = [(feat.at[r], xs.at[0, r]), (cot.at[r], g.at[r]), (tea.at[2, r], tb.at[2, r])]
        pairs += [(pre.at[i, r], pb.at[i, r]) for i in range(LAYERS)]
        loads.append([pltpu.make_async_copy(a, b, ld.at[c, n]) for n, (a, b) in enumerate(pairs)])
    for group in loads:
        for copy in group:
            copy.start()
    wload = [pltpu.make_async_copy(ker.at[i], w.at[i], ldw.at[i]) for i in range(LAYERS)]
    tload = [pltpu.make_async_copy(tea.at[i], tb.at[i], ldt.at[i]) for i in range(2)]
    wload[2].start()
    tload[1].start()
    wload[1].start()
    tload[0].start()
    wload[0].start()

    def missing(condition, ref):
        @pl.when(condition)
        def _():
            ref[...] = jnp.zeros((ROWS, C), F32)

    missing(jnp.logical_or(jnp.logical_and(low, me - 8 < 0), jnp.logical_and(z >= 2, me + 8 > last)), rb.at[2, 1])
    missing(me + 2 > last, rb.at[1, 0])
    missing(me - 2 < 0, rb.at[1, 1])
    missing(me + 1 > last, rb.at[0, 0])
    missing(me - 1 < 0, rb.at[0, 1])

    def shift(layer, way, c, src, target):
        return pltpu.make_async_remote_copy(
            src_ref=src.at[rows(c)],
            dst_ref=rb.at[layer, way, rows(c)],
            send_sem=ss.at[layer, way, c],
            recv_sem=rs.at[layer, way, c],
            device_id=(target,),
            device_id_type=MESH,
        )

    def strips(c, body):
        def step(n, carry):
            body(pl.ds(pl.multiple_of(c * CHUNK + n * STRIP, STRIP), STRIP))
            return carry

        lax.fori_loop(0, CHUNK // STRIP, step, 0)

    def first(r):
        state = xs[0, r]
        for i in range(2):
            p = pb[i, r]
            cdf = cdf_of(p)
            state = state + p * cdf
            xs[i + 1, r] = state
            pb[i, r] = cdf + p * density_of(p)
        p = pb[2, r]
        cdf = cdf_of(p)
        state = state + p * cdf
        grad = g[r] + MIMIC * (state - tb[2, r])
        g[r] = grad
        gu[2, r] = grad * (cdf + p * density_of(p))

    for c in range(CHUNKS):
        for copy in loads[c]:
            copy.wait()
        strips(c, first)
        if c == 0:
            pl.semaphore_wait(barrier, greeted)
        shift(2, 0, c, gu.at[2], across).start()

    def term(layer, k, ref):
        full = dot(xs[layer], ref[...], 0)
        for q in range(4):
            kg[layer, q, k] = full[:, q * 128 : (q + 1) * 128].reshape(SIDE, SIDE, STRIP, 128)

    def remote(src, dst, send, recv, target):
        return pltpu.make_async_remote_copy(
            src_ref=src, dst_ref=dst, send_sem=send, recv_sem=recv, device_id=(target,), device_id_type=MESH
        )

    def pair(layer, o, k):
        return remote(kg.at[layer, pl.ds(2 * (1 - core), 2), k], pbuf.at[layer, :, k], ps.at[layer, o], pr.at[layer, o], mate)

    def pair_sum(layer, o, k):
        pair(layer, o, k).wait()
        for ab in range(2):
            kg[layer, 2 * core + ab, k] = kg[layer, 2 * core + ab, k] + pbuf[layer, ab, k]

    def stage1(layer, o, k):
        copies = []
        for j in range(1, SIDE):
            copies.append(remote(
                kg.at[layer, 2 * core, k, :, (x + j) % SIDE], r1.at[layer, 0, j - 1, k],
                s1.at[layer, o, 0, j - 1], q1.at[layer, o, 0, j - 1], xp[j - 1]))
            copies.append(remote(
                kg.at[layer, 2 * core + 1, k, (y + j) % SIDE], r1.at[layer, 1, j - 1, k],
                s1.at[layer, o, 1, j - 1], q1.at[layer, o, 1, j - 1], yp[j - 1]))
        return copies

    def stage1_sum(layer, o, k):
        for copy in stage1(layer, o, k):
            copy.wait()
        t1[layer, 0, k] = kg[layer, 2 * core, k, :, x] + r1[layer, 0, 0, k] + r1[layer, 0, 1, k] + r1[layer, 0, 2, k]
        t1[layer, 1, k] = kg[layer, 2 * core + 1, k, y] + r1[layer, 1, 0, k] + r1[layer, 1, 1, k] + r1[layer, 1, 2, k]

    def stage2(layer):
        copies = []
        for j in range(1, SIDE):
            copies.append(remote(
                t1.at[layer, 0, :, (y + j) % SIDE], r2.at[layer, 0, j - 1],
                s2.at[layer, 0, j - 1], q2.at[layer, 0, j - 1], yp[j - 1]))
            copies.append(remote(
                t1.at[layer, 1, :, (x + j) % SIDE], r2.at[layer, 1, j - 1],
                s2.at[layer, 1, j - 1], q2.at[layer, 1, j - 1], xp[j - 1]))
        return copies

    def stage2_sum(layer):
        for copy in stage2(layer):
            copy.wait()
        for ab, at in ((0, y), (1, x)):
            total = t1[layer, ab, :, at] + r2[layer, ab, 0] + r2[layer, ab, 1] + r2[layer, ab, 2]
            u[layer, ab] = total.reshape(TAPS, SIDE, 8, 128)

    def stage3(layer):
        return [
            remote(u.at[layer, :, :, (z + j) % SIDE], r3.at[layer, j - 1], s3.at[layer, j - 1], q3.at[layer, j - 1], zp[j - 1])
            for j in range(1, SIDE)
        ]

    def stage3_sum(layer):
        for copy in stage3(layer):
            copy.wait()
        v[layer] = (u[layer, :, :, z] + r3[layer, 0] + r3[layer, 1] + r3[layer, 2]) * SCALE

    def stage4(layer):
        return [remote(v.at[layer], r4.at[layer], s4.at[layer], q4.at[layer], mate)]

    def finish(layer):
        for copy in stage4(layer):
            copy.wait()
        for ab in range(2):
            for k in range(TAPS):
                mine, other = v[layer, ab, k], r4[layer, ab, k]
                for half in range(2):
                    whole = jnp.where(core == half, mine, other)
                    q = 2 * half + ab
                    kgrad[layer, k, :, q * 128 : (q + 1) * 128] = jnp.where(core == 0, whole[:4], whole[4:])

    def go(copies):
        for copy in copies:
            copy.start()

    near = jnp.where(low, 0, 2)
    far = 2 - near
    wload[2].wait()
    g[...] = g[...] + dot(gu[2], w[2, 1], 1)
    term(2, 1, gu.at[2])
    pair(2, 0, 1).start()
    tload[1].wait()

    forwards = jnp.logical_and(forward >= 0, forward <= last)
    fed = jnp.logical_and(source >= 0, source <= last)

    def swapped(c):
        shift(2, 0, c, gu.at[2], across).wait_recv()

        @pl.when(forwards)
        def _():
            shift(2, 1, c, rb.at[2, 0], forward).start()

        g[rows(c)] = g[rows(c)] + dot(rb[2, 0, rows(c)], w[2, near], 1)

    def send(layer, c):
        step = 2**layer

        @pl.when(me - step >= 0)
        def _():
            shift(layer, 0, c, gu.at[layer], me - step).start()

        @pl.when(me + step <= last)
        def _():
            shift(layer, 1, c, gu.at[layer], me + step).start()

    def arrive(layer, c):
        step = 2**layer

        @pl.when(me + step <= last)
        def _():
            shift(layer, 0, c, gu.at[layer], me).wait_recv()

        @pl.when(me - step >= 0)
        def _():
            shift(layer, 1, c, gu.at[layer], me).wait_recv()

    def sent(layer, c):
        step = 2**layer

        @pl.when(me - step >= 0)
        def _():
            shift(layer, 0, c, gu.at[layer], me - step).wait_send()

        @pl.when(me + step <= last)
        def _():
            shift(layer, 1, c, gu.at[layer], me + step).wait_send()

    def next_gu(layer, c):
        def body(r):
            grad = g[r] + MIMIC * (xs[layer + 1, r] - tb[layer, r])
            g[r] = grad
            gu[layer, r] = grad * pb[layer, r]

        strips(c, body)
        send(layer, c)

    def forwarded(c):
        @pl.when(fed)
        def _():
            shift(2, 1, c, rb.at[2, 0], forward).wait_recv()

        g[rows(c)] = g[rows(c)] + dot(rb[2, 1, rows(c)], w[2, far], 1)
        next_gu(1, c)

    swapped(0)
    swapped(1)
    forwarded(0)
    swapped(2)
    forwarded(1)
    swapped(3)
    forwarded(2)
    forwarded(3)
    for c in range(CHUNKS):
        shift(2, 0, c, gu.at[2], across).wait_send()

        @pl.when(forwards)
        def _():
            shift(2, 1, c, rb.at[2, 0], forward).wait_send()

    term(2, near, rb.at[2, 0])
    pair(2, 1, near).start()
    term(2, far, rb.at[2, 1])
    pair(2, 2, far).start()
    pair_sum(2, 0, 1)
    go(stage1(2, 0, 1))

    wload[1].wait()
    tload[0].wait()
    g[...] = g[...] + dot(gu[1], w[1, 1], 1)
    pair_sum(2, 1, near)
    go(stage1(2, 1, near))
    term(1, 1, gu.at[1])
    pair(1, 0, 1).start()
    pair_sum(2, 2, far)
    go(stage1(2, 2, far))
    for c in range(CHUNKS):
        arrive(1, c)
        g[rows(c)] = g[rows(c)] + dot(rb[1, 0, rows(c)], w[1, 0], 1) + dot(rb[1, 1, rows(c)], w[1, 2], 1)
        next_gu(0, c)
        if c == 1:
            stage1_sum(2, 0, 1)
            stage1_sum(2, 1, near)
            stage1_sum(2, 2, far)
            go(stage2(2))
        if c == 2:
            stage2_sum(2)
            go(stage3(2))
    for c in range(CHUNKS):
        sent(1, c)
    term(1, 0, rb.at[1, 0])
    pair(1, 1, 0).start()
    term(1, 2, rb.at[1, 1])
    pair(1, 2, 2).start()
    pair_sum(1, 0, 1)
    go(stage1(1, 0, 1))
    stage3_sum(2)
    go(stage4(2))

    wload[0].wait()
    term(0, 1, gu.at[0])
    pair(0, 0, 1).start()
    pair_sum(1, 1, 0)
    go(stage1(1, 1, 0))
    pair_sum(1, 2, 2)
    go(stage1(1, 2, 2))
    g[...] = g[...] + dot(gu[0], w[0, 1], 1)
    pair_sum(0, 0, 1)
    go(stage1(0, 0, 1))
    for c in range(CHUNKS):
        arrive(0, c)
        if c < CHUNKS - 1:
            g[rows(c)] = g[rows(c)] + dot(rb[0, 0, rows(c)], w[0, 0], 1) + dot(rb[0, 1, rows(c)], w[0, 2], 1)
    term(0, 0, rb.at[0, 0])
    pair(0, 1, 0).start()
    term(0, 2, rb.at[0, 1])
    pair(0, 2, 2).start()
    finish(2)
    pair_sum(0, 1, 0)
    go(stage1(0, 1, 0))
    pair_sum(0, 2, 2)
    go(stage1(0, 2, 2))
    c = CHUNKS - 1
    g[rows(c)] = g[rows(c)] + dot(rb[0, 0, rows(c)], w[0, 0], 1) + dot(rb[0, 1, rows(c)], w[0, 2], 1)
    out[...] = g[...]
    for o, k in enumerate((1, 0, 2)):
        stage1_sum(1, o, k)
    go(stage2(1))
    for o, k in enumerate((1, 0, 2)):
        stage1_sum(0, o, k)
    go(stage2(0))
    stage2_sum(1)
    go(stage3(1))
    stage2_sum(0)
    go(stage3(0))
    stage3_sum(1)
    go(stage4(1))
    stage3_sum(0)
    go(stage4(0))
    for c in range(CHUNKS):
        sent(0, c)
    finish(1)
    finish(0)


def shards(features, preacts, teacher, cotangent, kernels):
    vmem = lambda *shape: pltpu.VMEM(shape, F32)
    dma = lambda *shape: pltpu.SemaphoreType.DMA(shape)
    return pl.pallas_call(
        kernel,
        out_shape=(
            jax.ShapeDtypeStruct((ROWS, C), F32),
            jax.ShapeDtypeStruct((LAYERS, TAPS, 4, C), F32),
        ),
        in_specs=[pl.BlockSpec(memory_space=pl.ANY)] * 5,
        out_specs=(pl.BlockSpec(memory_space=pltpu.VMEM), pl.BlockSpec(memory_space=pltpu.VMEM)),
        scratch_shapes=[
            vmem(LAYERS, ROWS, C),
            vmem(LAYERS, ROWS, C),
            vmem(LAYERS, ROWS, C),
            vmem(ROWS, C),
            vmem(LAYERS, ROWS, C),
            vmem(LAYERS, 2, ROWS, C),
            vmem(LAYERS, TAPS, C, C),
            vmem(LAYERS, 4, TAPS, SIDE, SIDE, STRIP, 128),
            vmem(LAYERS, 2, TAPS, SIDE, SIDE, STRIP, 128),
            vmem(LAYERS, 2, 3, TAPS, SIDE, STRIP, 128),
            vmem(LAYERS, 2, TAPS, SIDE, STRIP, 128),
            vmem(LAYERS, 2, 3, TAPS, STRIP, 128),
            vmem(LAYERS, 2, TAPS, SIDE, 8, 128),
            vmem(LAYERS, 3, 2, TAPS, 8, 128),
            vmem(LAYERS, 2, TAPS, 8, 128),
            vmem(LAYERS, 2, TAPS, 8, 128),
            dma(CHUNKS, 6), dma(2), dma(LAYERS),
            dma(LAYERS, 2, CHUNKS), dma(LAYERS, 2, CHUNKS),
            dma(LAYERS, 3), dma(LAYERS, 3),
            dma(LAYERS, 3, 2, 3), dma(LAYERS, 3, 2, 3),
            dma(LAYERS, 2, 3), dma(LAYERS, 2, 3),
            dma(LAYERS, 3), dma(LAYERS, 3),
            dma(LAYERS), dma(LAYERS),
        ],
        name="distill",
        compiler_params=pltpu.CompilerParams(collective_id=0, has_side_effects=True, vmem_limit_bytes=61 * 1024 * 1024),
    )(features, preacts, teacher, cotangent, kernels)


def solution(mesh):
    in_specs = (P("seq", None), P(None, "seq", None), P(None, "seq", None), P("seq", None), P())
    out_specs = (P("seq", None), P(None, None, "seq", None))
    return jax.shard_map(shards, mesh=mesh, in_specs=in_specs, out_specs=out_specs, check_vma=False)
```

profile of v0, /device:TPU:1, one launch (start us, length us, event | category | flops | bytes accessed | tf_op | source)
XLA Modules:
  0.0 115.2 jit_solution(4500028943212467583)
XLA Ops:
  0.6 110.7 %distill.1 = (f32[512,512]{1,0:T(8,128)}, f32[3,3,4,512]{3,2,1,0:T(4,128)}) custom-call(f32[512,512]{1,0:T(8,128)} %feat.1, f32[3,512,512]{2,1,0:T(8,128)} %pre.1, f32[3,512,512]{2,1,0:T(8,128)} %tea.1, f32[512,512]{1,0:T(8,128)} %cot.1, f32[3,3,512,512]{3,2,1,0:T(8,128)} %ker.1), custom_call_target="tpu_custom_call" | custom-call | tf_op jit(solution)/shard_map/distill/pallas_call | solution.py:403
  111.4 2.3 %copy.9 = f32[512,512]{1,0:T(8,128)} copy(f32[512,512]{1,0:T(8,128)} %get-tuple-element.4) | data formatting | bytes 2097152
  113.6 1.5 %copy.10 = f32[3,3,4,512]{3,2,1,0:T(4,128)} copy(f32[3,3,4,512]{3,2,1,0:T(4,128)} %get-tuple-element.5) | data formatting | bytes 147456
where the time goes:
time: 115 us
  Pallas kernels  111 us (97%)
  local copies, waits for them, and re-layouts  3.78 us (3%)
    pallas_call x1, Pallas kernels, shards(): pl.pallas_call(kernel, out_shape=(jax.ShapeDtypeStruct((ROWS, C), F32), j...  111 us
    unnamed x2, local copies, waits for them, and re-layouts  3.78 us

commit v1 on v0

v1 whole, which is shorter than its diff:
```python
import math

import jax
import jax.numpy as jnp
from jax import lax
from jax.experimental import pallas as pl
from jax.experimental.pallas import tpu as pltpu
from jax.sharding import PartitionSpec as P

LAYERS = 3
TAPS = 3
SIDE = 4
ROWS = 512
C = 512
CHUNKS = 4
CHUNK = ROWS // CHUNKS
STRIP = 32
SCALE = 1.0 / math.sqrt(65536)
MIMIC = 0.5
MESH = pl.DeviceIdType.MESH
F32 = jnp.float32
LIMIT = 61 * 1024 * 1024
PARTS = 4


def cdf_of(u):
    return 0.5 * (1.0 + lax.erf(u * (1.0 / math.sqrt(2.0))))


def density_of(u):
    return jnp.exp(-0.5 * u * u) * (1.0 / math.sqrt(2.0 * math.pi))


def dot(left, right, over):
    return lax.dot_general(
        left, right, (((over,), (over,)), ((), ())), precision=lax.Precision.HIGH, preferred_element_type=F32
    )


def kernel(
    feat, pre, tea, cot, ker, out, kgrad,
    xs, pb, tb, g, gu, rb, w, kg, pbuf, r1, t1, r2, t2, r3, v, r4,
    go_sem, ld, ldt, ldw, ss, rs, ps, pr, q1, q2, q3, s4, q4,
):
    me = lax.axis_index("seq")
    core = me % 2
    z = (me // 2) % SIDE
    x = (me // 8) % SIDE
    y = me // 32
    last = 127

    def device(yy, xx, zz):
        return ((yy * SIDE + xx) * SIDE + zz) * 2 + core

    mate = me + 1 - 2 * core
    across = device(y, x, (z + 2) % SIDE)
    low = z < 2
    forward = jnp.where(low, me + 8, me - 8)
    source = jnp.where(low, me - 8, me + 8)
    xp = [device(y, (x + j) % SIDE, z) for j in range(1, SIDE)]
    yp = [device((y + j) % SIDE, x, z) for j in range(1, SIDE)]
    zp = [device(y, x, (z + j) % SIDE) for j in range(1, SIDE)]

    barrier = pltpu.get_barrier_semaphore()
    always = [mate, *xp, *yp, *zp]
    for other in always:
        pl.semaphore_signal(barrier, inc=1, device_id=(other,), device_id_type=MESH)
    greeted = len(always)
    for by, ring in ((1, 2), (-1, 2), (2, 8), (-2, 8), (8, 32), (-8, 32)):
        there = jnp.logical_and(me % ring + by < 0, me + by >= 0)
        if by > 0:
            there = jnp.logical_and(me % ring + by >= ring, me + by <= last)

        @pl.when(there)
        def _():
            pl.semaphore_signal(barrier, inc=1, device_id=(me + by,), device_id_type=MESH)

        greeted = greeted + jnp.where(there, 1, 0)

    def rows(c):
        return pl.ds(c * CHUNK, CHUNK)

    loads = []
    for c in range(CHUNKS):
        r = rows(c)
        pairs = [(feat.at[r], xs.at[0, r]), (cot.at[r], g.at[r]), (tea.at[2, r], tb.at[2, r])]
        pairs += [(pre.at[i, r], pb.at[i, r]) for i in range(LAYERS)]
        loads.append([pltpu.make_async_copy(a, b, ld.at[c, n]) for n, (a, b) in enumerate(pairs)])
    for group in loads:
        for copy in group:
            copy.start()
    wload = [pltpu.make_async_copy(ker.at[i], w.at[i], ldw.at[i]) for i in range(LAYERS)]
    tload = [pltpu.make_async_copy(tea.at[i], tb.at[i], ldt.at[i]) for i in range(2)]
    wload[2].start()
    tload[1].start()
    wload[1].start()
    tload[0].start()
    wload[0].start()

    def missing(condition, ref):
        @pl.when(condition)
        def _():
            ref[...] = jnp.zeros((ROWS, C), F32)

    missing(jnp.logical_or(jnp.logical_and(low, me - 8 < 0), jnp.logical_and(z >= 2, me + 8 > last)), rb.at[2, 1])
    missing(me + 2 > last, rb.at[1, 0])
    missing(me - 2 < 0, rb.at[1, 1])
    missing(me + 1 > last, rb.at[0, 0])
    missing(me - 1 < 0, rb.at[0, 1])

    def shift(layer, way, c, src, target):
        return pltpu.make_async_remote_copy(
            src_ref=src.at[rows(c)],
            dst_ref=rb.at[layer, way, rows(c)],
            send_sem=ss.at[layer, way, c],
            recv_sem=rs.at[layer, way, c],
            device_id=(target,),
            device_id_type=MESH,
        )

    def strips(c, body):
        def step(n, carry):
            body(pl.ds(pl.multiple_of(c * CHUNK + n * STRIP, STRIP), STRIP))
            return carry

        lax.fori_loop(0, CHUNK // STRIP, step, 0)

    def first(r):
        state = xs[0, r]
        for i in range(2):
            p = pb[i, r]
            cdf = cdf_of(p)
            state = state + p * cdf
            xs[i + 1, r] = state
            pb[i, r] = cdf + p * density_of(p)
        p = pb[2, r]
        cdf = cdf_of(p)
        state = state + p * cdf
        grad = g[r] + MIMIC * (state - tb[2, r])
        g[r] = grad
        gu[2, r] = grad * (cdf + p * density_of(p))

    for c in range(CHUNKS):
        for copy in loads[c]:
            copy.wait()
        strips(c, first)
        if c == 0:
            pl.semaphore_wait(barrier, greeted)
        shift(2, 0, c, gu.at[2], across).start()

    def place(layer, q, k, value, add=False):
        value = value.reshape(SIDE, SIDE, SIDE, 8, 128)
        kg[layer, q, k] = kg[layer, q, k] + value if add else value

    def term(layer, k, ref, rows_of=slice(None), add=False):
        full = dot(xs[layer, rows_of], ref[rows_of], 0)
        for q in range(4):
            place(layer, q, k, full[:, q * 128 : (q + 1) * 128], add)

    def lanes(q):
        return pl.ds(q * 128, 128)

    def term_of_columns(k, ref, ab):
        both = dot(xs[0], jnp.concatenate([ref[:, lanes(ab)], ref[:, lanes(2 + ab)]], axis=1), 0)
        place(0, ab, k, both[:, :128])
        place(0, 2 + ab, k, both[:, 128:])

    def remote(src, dst, send, recv, target):
        return pltpu.make_async_remote_copy(
            src_ref=src, dst_ref=dst, send_sem=send, recv_sem=recv, device_id=(target,), device_id_type=MESH
        )

    where = {"x": x, "y": y, "z": z}
    peers = {"x": xp, "y": yp, "z": zp}

    def pair(layer, k, ab):
        return remote(kg.at[layer, 2 * (1 - core) + ab, k], pbuf.at[layer, ab, k], ps.at[layer, k, ab], pr.at[layer, k, ab], mate)

    def pair_sum(layer, k, ab):
        pair(layer, k, ab).wait()
        kg[layer, 2 * core + ab, k] = kg[layer, 2 * core + ab, k] + pbuf[layer, ab, k]

    def cut(n, layer, k, ab, path, at):
        held = (kg.at[layer, 2 * core + ab, k], t1.at[layer, ab, k], t2.at[layer, ab, k])[n]
        left = [axis for axis in "yxz" if axis not in path[:n]]
        return held.at[tuple(at if axis == path[n] else slice(None) for axis in left)]

    def stage(n, layer, k, ab, path):
        axis = path[n]
        return [
            remote(
                cut(n, layer, k, ab, path, (where[axis] + j) % SIDE), (r1, r2, r3)[n].at[layer, ab, k, j - 1],
                ps.at[layer, k, ab], (q1, q2, q3)[n].at[layer, k, ab], peers[axis][j - 1])
            for j in range(1, SIDE)
        ]

    def stage_sum(n, layer, k, ab, path):
        got = (r1, r2, r3)[n]
        all3 = got.at[layer, ab, k]
        remote(all3, all3, ps.at[layer, k, ab], (q1, q2, q3)[n].at[layer, k, ab], mate).wait()
        own = cut(n, layer, k, ab, path, where[path[n]])[...]
        total = own + got[layer, ab, k, 0] + got[layer, ab, k, 1] + got[layer, ab, k, 2]
        if n < 2:
            (t1, t2)[n][layer, ab, k] = total
        else:
            v[layer, ab, k] = total * SCALE

    def stage4(layer, ab):
        return [remote(v.at[layer, ab], r4.at[layer, ab], s4.at[layer, ab], q4.at[layer, ab], mate)]

    def finish(layer, ab):
        for copy in stage4(layer, ab):
            copy.wait()
        for k in range(TAPS):
            mine, other = v[layer, ab, k], r4[layer, ab, k]
            for half in range(2):
                whole = jnp.where(core == half, mine, other)
                kgrad[layer, k, :4, lanes(2 * half + ab)] = jnp.where(core == 0, whole[:4], whole[4:])

    def go(copies):
        for copy in copies:
            copy.start()

    def send_pair(layer, k, halves=(0, 1)):
        go([pair(layer, k, ab) for ab in halves])

    def start1(layer, units):
        for unit in units:
            pair_sum(layer, *unit[:2])
            go(stage(0, layer, *unit))

    def start2(layer, units):
        for unit in units:
            stage_sum(0, layer, *unit)
            go(stage(1, layer, *unit))

    def start3(layer, units):
        for unit in units:
            stage_sum(1, layer, *unit)
            go(stage(2, layer, *unit))

    def start4(layer, units):
        for ab in range(2):
            mine = [unit for unit in units if unit[1] == ab]
            for unit in mine:
                stage_sum(2, layer, *unit)
            if mine:
                go(stage4(layer, ab))

    near = jnp.where(low, 0, 2)
    far = 2 - near
    wload[2].wait()
    g[...] = g[...] + dot(gu[2], w[2, 1], 1)
    term(2, 1, gu.at[2])
    send_pair(2, 1)
    tload[1].wait()

    forwards = jnp.logical_and(forward >= 0, forward <= last)
    fed = jnp.logical_and(source >= 0, source <= last)

    def swapped(c):
        shift(2, 0, c, gu.at[2], across).wait_recv()

        @pl.when(forwards)
        def _():
            shift(2, 1, c, rb.at[2, 0], forward).start()

        g[rows(c)] = g[rows(c)] + dot(rb[2, 0, rows(c)], w[2, near], 1)

    def send(layer, c):
        step = 2**layer

        @pl.when(me - step >= 0)
        def _():
            shift(layer, 0, c, gu.at[layer], me - step).start()

        @pl.when(me + step <= last)
        def _():
            shift(layer, 1, c, gu.at[layer], me + step).start()

    def arrive(layer, c):
        step = 2**layer

        @pl.when(me + step <= last)
        def _():
            shift(layer, 0, c, gu.at[layer], me).wait_recv()

        @pl.when(me - step >= 0)
        def _():
            shift(layer, 1, c, gu.at[layer], me).wait_recv()

    def sent(layer, c):
        step = 2**layer

        @pl.when(me - step >= 0)
        def _():
            shift(layer, 0, c, gu.at[layer], me - step).wait_send()

        @pl.when(me + step <= last)
        def _():
            shift(layer, 1, c, gu.at[layer], me + step).wait_send()

    def next_gu(layer, c):
        def body(r):
            grad = g[r] + MIMIC * (xs[layer + 1, r] - tb[layer, r])
            g[r] = grad
            gu[layer, r] = grad * pb[layer, r]

        strips(c, body)

    def forwarded(c):
        @pl.when(fed)
        def _():
            shift(2, 1, c, rb.at[2, 0], forward).wait_recv()

        g[rows(c)] = g[rows(c)] + dot(rb[2, 1, rows(c)], w[2, far], 1)
        next_gu(1, c)

    units2 = [(k, ab, ("xyz", "yxz")[ab]) for k in (1, near, far) for ab in range(2)]
    start1(2, units2[:2])
    for c in range(CHUNKS + 1):
        if c < CHUNKS:
            swapped(c)
        if c == CHUNKS:
            term(2, near, rb.at[2, 0])
            send_pair(2, near)
        if c >= 1:
            forwarded(c - 1)
            if c >= CHUNKS - 2:
                send(1, c - 2)
            if c == CHUNKS:
                send(1, c - 1)
    term(2, far, rb.at[2, 1])
    send_pair(2, far)
    start1(2, units2[2:4])
    for c in range(CHUNKS):
        shift(2, 0, c, gu.at[2], across).wait_send()

        @pl.when(forwards)
        def _():
            shift(2, 1, c, rb.at[2, 0], forward).wait_send()

    wload[1].wait()
    tload[0].wait()
    g[...] = g[...] + dot(gu[1], w[1, 1], 1)
    term(1, 1, gu.at[1])
    send_pair(1, 1)
    start1(2, units2[4:])
    half = (slice(0, ROWS // 2), slice(ROWS // 2, ROWS))
    for c in range(CHUNKS):
        arrive(1, c)
        g[rows(c)] = g[rows(c)] + dot(rb[1, 0, rows(c)], w[1, 0], 1) + dot(rb[1, 1, rows(c)], w[1, 2], 1)
        next_gu(0, c)
        if c == 1:
            term(1, 0, rb.at[1, 0], half[0])
            term(1, 2, rb.at[1, 1], half[0])

    def across_chip(way, q):
        return remote(
            gu.at[0, :, lanes(q)], rb.at[0, way, :, lanes(q)], ss.at[0, way, q], rs.at[0, way, q], me - 1 if way == 0 else me + 1
        )

    order = ((0, 2), (1, 3))

    def each_way(groups, method):
        for q in groups:
            for way in range(2):
                here = (me - 1 >= 0) if way == 0 else (me + 1 <= last)
                if method == "wait_recv":
                    here = (me + 1 <= last) if way == 0 else (me - 1 >= 0)

                @pl.when(here)
                def _():
                    getattr(across_chip(way, q), method)()

    for groups in order:
        each_way(groups, "start")
    term(1, 0, rb.at[1, 0], half[1], True)
    send_pair(1, 0)
    term(1, 2, rb.at[1, 1], half[1], True)
    send_pair(1, 2)
    for c in range(CHUNKS):
        sent(1, c)
    wload[0].wait()
    term(0, 1, gu.at[0])
    send_pair(0, 1)
    units1 = [(0, 0, "xyz"), (0, 1, "yxz"), (2, 0, "xyz"), (2, 1, "yxz"), (1, 0, "zxy"), (1, 1, "zyx")]
    units0 = [(1, 0, "zxy"), (1, 1, "zyx"), (0, 0, "xyz"), (2, 0, "yxz"), (0, 1, "zxy"), (2, 1, "yxz")]
    start1(1, units1)
    start1(0, units0[:2])
    g[...] = g[...] + dot(gu[0], w[0, 1], 1)
    for ab, groups in enumerate(order):
        if ab == 1:
            start2(2, units2)
        each_way(groups, "wait_recv")
        term_of_columns(0, rb.at[0, 0], ab)
        send_pair(0, 0, (ab,))
        term_of_columns(2, rb.at[0, 1], ab)
        send_pair(0, 2, (ab,))
        if ab == 1:
            g[...] = g[...] + dot(rb[0, 0], w[0, 0], 1)
        start1(0, units0[2 + 2 * ab : 4 + 2 * ab])
    start3(2, units2)
    g[...] = g[...] + dot(rb[0, 1], w[0, 2], 1)
    start2(1, units1)
    start4(2, units2)
    result = pltpu.make_async_copy(g, out, go_sem)
    result.start()
    start2(0, units0[:4])
    start3(1, units1)
    start2(0, units0[4:])
    start3(0, units0[:4])
    start4(1, units1)
    finish(2, 0)
    finish(2, 1)
    start3(0, units0[4:])
    for groups in order:
        each_way(groups, "wait_send")
    start4(0, units0)
    finish(1, 0)
    finish(1, 1)
    finish(0, 0)
    finish(0, 1)
    result.wait()


def hand_over(grad, blocks, grad_out, kernel_grad_out, held, held_blocks, taken, given):
    part = ROWS // PARTS
    takes, gives = [], []
    for n in range(PARTS):
        r = pl.ds(n * part, part)
        takes.append(pltpu.make_async_copy(grad.at[r], held.at[r], taken.at[n]))
        gives.append(pltpu.make_async_copy(held.at[r], grad_out.at[r], given.at[n]))
    takes.append(pltpu.make_async_copy(blocks, held_blocks, taken.at[PARTS]))
    for copy in takes:
        copy.start()
    for n in range(PARTS):
        takes[n].wait()
        gives[n].start()
    takes[PARTS].wait()
    kernel_grad_out[...] = held_blocks[:, :, :4]
    for copy in gives:
        copy.wait()


def shards(features, preacts, teacher, cotangent, kernels):
    vmem = lambda *shape: pltpu.VMEM(shape, F32)
    dma = lambda *shape: pltpu.SemaphoreType.DMA(shape)
    grad, blocks = pl.pallas_call(
        kernel,
        out_shape=(
            jax.ShapeDtypeStruct((ROWS, C), F32),
            jax.ShapeDtypeStruct((LAYERS, TAPS, 8, C), F32),
        ),
        in_specs=[pl.BlockSpec(memory_space=pl.ANY)] * 5,
        out_specs=(pl.BlockSpec(memory_space=pl.ANY), pl.BlockSpec(memory_space=pltpu.VMEM)),
        scratch_shapes=[
            vmem(LAYERS, ROWS, C),
            vmem(LAYERS, ROWS, C),
            vmem(LAYERS, ROWS, C),
            vmem(ROWS, C),
            vmem(LAYERS, ROWS, C),
            vmem(LAYERS, 2, ROWS, C),
            vmem(LAYERS, TAPS, C, C),
            vmem(LAYERS, 4, TAPS, SIDE, SIDE, SIDE, 8, 128),
            vmem(LAYERS, 2, TAPS, SIDE, SIDE, SIDE, 8, 128),
            vmem(LAYERS, 2, TAPS, 3, SIDE, SIDE, 8, 128),
            vmem(LAYERS, 2, TAPS, SIDE, SIDE, 8, 128),
            vmem(LAYERS, 2, TAPS, 3, SIDE, 8, 128),
            vmem(LAYERS, 2, TAPS, SIDE, 8, 128),
            vmem(LAYERS, 2, TAPS, 3, 8, 128),
            vmem(LAYERS, 2, TAPS, 8, 128),
            vmem(LAYERS, 2, TAPS, 8, 128),
            pltpu.SemaphoreType.DMA, dma(CHUNKS, 6), dma(2), dma(LAYERS),
            dma(LAYERS, 2, CHUNKS), dma(LAYERS, 2, CHUNKS),
            dma(LAYERS, 3, 2), dma(LAYERS, 3, 2),
            dma(LAYERS, 3, 2), dma(LAYERS, 3, 2), dma(LAYERS, 3, 2),
            dma(LAYERS, 2), dma(LAYERS, 2),
        ],
        name="distill",
        compiler_params=pltpu.CompilerParams(collective_id=0, has_side_effects=True, vmem_limit_bytes=LIMIT),
    )(features, preacts, teacher, cotangent, kernels)
    return pl.pallas_call(
        hand_over,
        out_shape=(
            jax.ShapeDtypeStruct((ROWS, C), F32),
            jax.ShapeDtypeStruct((LAYERS, TAPS, 4, C), F32),
        ),
        in_specs=[pl.BlockSpec(memory_space=pl.ANY)] * 2,
        out_specs=(pl.BlockSpec(memory_space=pl.ANY), pl.BlockSpec(memory_space=pltpu.VMEM)),
        scratch_shapes=[vmem(ROWS, C), vmem(LAYERS, TAPS, 8, C), dma(PARTS + 1), dma(PARTS)],
        name="hand_over",
        compiler_params=pltpu.CompilerParams(vmem_limit_bytes=LIMIT),
    )(grad, blocks)


def solution(mesh):
    in_specs = (P("seq", None), P(None, "seq", None), P(None, "seq", None), P("seq", None), P())
    out_specs = (P("seq", None), P(None, None, "seq", None))
    return jax.shard_map(shards, mesh=mesh, in_specs=in_specs, out_specs=out_specs, check_vma=False)
```

time: 115 us -> 109 us (0.948)
  local copies, waits for them, and re-layouts: 3.78 us -> 0 us
  Pallas kernels: 111 us -> 108 us
    pallas_call x1, Pallas kernels: 111 us -> 105 us  [shards(): pl.pallas_call(kernel, out_shape=(jax.ShapeDtypeStruct((ROWS, C), F32), j...]
    unnamed x2 -> x0, local copies, waits for them, and re-layouts: 3.78 us -> none
    pallas_call x0 -> x1, Pallas kernels: none -> 2.62 us  [shards(): pl.pallas_call(hand_over, out_shape=(jax.ShapeDtypeStruct((ROWS, C), F32)...]
where the time goes in v1:
time: 109 us
  Pallas kernels  108 us (99%)
    pallas_call x1, Pallas kernels, shards(): pl.pallas_call(kernel, out_shape=(jax.ShapeDtypeStruct((ROWS, C), F32), j...  105 us
    pallas_call x1, Pallas kernels, shards(): pl.pallas_call(hand_over, out_shape=(jax.ShapeDtypeStruct((ROWS, C), F32)...  2.62 us

profile of v1, /device:TPU:1, one launch (start us, length us, event | category | flops | bytes accessed | tf_op | source)
XLA Modules:
  0.0 108.8 jit_solution(1589261543611969377)
XLA Ops:
  0.6 105.4 %distill.1 = (f32[512,512]{1,0:T(8,128)}, f32[3,3,8,512]{3,2,1,0:T(8,128)}) custom-call(f32[512,512]{1,0:T(8,128)} %feat.1, f32[3,512,512]{2,1,0:T(8,128)} %pre.1, f32[3,512,512]{2,1,0:T(8,128)} %tea.1, f32[512,512]{1,0:T(8,128)} %cot.1, f32[3,3,512,512]{3,2,1,0:T(8,128)} %ker.1), custom_call_target="tpu_custom_call" | custom-call | tf_op jit(solution)/shard_map/distill/pallas_call | solution.py:449
  106.0 2.6 %hand_over.1 = (f32[512,512]{1,0:T(8,128)}, f32[3,3,4,512]{3,2,1,0:T(4,128)}) custom-call(f32[512,512]{1,0:T(8,128)} %get-tuple-element.4.grad, f32[3,3,8,512]{3,2,1,0:T(8,128)} %get-tuple-element.5.blocks), custom_call_target="tpu_custom_call" | custom-call | tf_op jit(solution)/shard_map/hand_over/pallas_call | solution.py:483

commit v2 on v1

--- a/solution.py
+++ b/solution.py
@@ -15,6 +15,7 @@
 CHUNKS = 4
 CHUNK = ROWS // CHUNKS
 STRIP = 32
+EARLY = 2
 SCALE = 1.0 / math.sqrt(65536)
 MIMIC = 0.5
 MESH = pl.DeviceIdType.MESH
@@ -40,7 +41,7 @@
 def kernel(
     feat, pre, tea, cot, ker, out, kgrad,
     xs, pb, tb, g, gu, rb, w, kg, pbuf, r1, t1, r2, t2, r3, v, r4,
-    go_sem, ld, ldt, ldw, ss, rs, ps, pr, q1, q2, q3, s4, q4,
+    go_sem, ld, ldt, ldw, ss, rs, cs, cr, ps, pr, q1, q2, q3, s4, q4,
 ):
     me = lax.axis_index("seq")
     core = me % 2
@@ -112,8 +113,8 @@
         return pltpu.make_async_remote_copy(
             src_ref=src.at[rows(c)],
             dst_ref=rb.at[layer, way, rows(c)],
-            send_sem=ss.at[layer, way, c],
-            recv_sem=rs.at[layer, way, c],
+            send_sem=ss.at[layer - 1, way, c],
+            recv_sem=rs.at[layer - 1, way, c],
             device_id=(target,),
             device_id_type=MESH,
         )
@@ -316,7 +317,7 @@
         g[rows(c)] = g[rows(c)] + dot(rb[2, 1, rows(c)], w[2, far], 1)
         next_gu(1, c)
 
-    units2 = [(k, ab, ("xyz", "yxz")[ab]) for k in (1, near, far) for ab in range(2)]
+    units2 = [(1, 0, "xyz"), (1, 1, "yxz"), (near, 0, "yxz"), (near, 1, "yxz"), (far, 0, "xyz"), (far, 1, "yxz")]
     start1(2, units2[:2])
     for c in range(CHUNKS + 1):
         if c < CHUNKS:
@@ -346,6 +347,26 @@
     term(1, 1, gu.at[1])
     send_pair(1, 1)
     start1(2, units2[4:])
+    def across_chip(way, q, n):
+        r = pl.ds(n * (ROWS // 2), ROWS // 2)
+        return remote(
+            gu.at[0, r, lanes(q)], rb.at[0, way, r, lanes(q)], cs.at[way, q, n], cr.at[way, q, n], me - 1 if way == 0 else me + 1
+        )
+
+    order = ((0, 2), (1, 3))
+
+    def each_way(groups, method, parts=(0, 1)):
+        for q in groups:
+            for way in range(2):
+                here = (me - 1 >= 0) if way == 0 else (me + 1 <= last)
+                if method == "wait_recv":
+                    here = (me + 1 <= last) if way == 0 else (me - 1 >= 0)
+
+                @pl.when(here)
+                def _():
+                    for n in parts:
+                        getattr(across_chip(way, q, n), method)()
+
     half = (slice(0, ROWS // 2), slice(ROWS // 2, ROWS))
     for c in range(CHUNKS):
         arrive(1, c)
@@ -354,27 +375,11 @@
         if c == 1:
             term(1, 0, rb.at[1, 0], half[0])
             term(1, 2, rb.at[1, 1], half[0])
-
-    def across_chip(way, q):
-        return remote(
-            gu.at[0, :, lanes(q)], rb.at[0, way, :, lanes(q)], ss.at[0, way, q], rs.at[0, way, q], me - 1 if way == 0 else me + 1
-        )
-
-    order = ((0, 2), (1, 3))
-
-    def each_way(groups, method):
-        for q in groups:
-            for way in range(2):
-                here = (me - 1 >= 0) if way == 0 else (me + 1 <= last)
-                if method == "wait_recv":
-                    here = (me + 1 <= last) if way == 0 else (me - 1 >= 0)
-
-                @pl.when(here)
-                def _():
-                    getattr(across_chip(way, q), method)()
-
-    for groups in order:
-        each_way(groups, "start")
+        if c == EARLY:
+            each_way(order[0], "start", (0,))
+
+    each_way(order[0], "start", (1,))
+    each_way(order[1], "start")
     term(1, 0, rb.at[1, 0], half[1], True)
     send_pair(1, 0)
     term(1, 2, rb.at[1, 1], half[1], True)
@@ -384,8 +389,8 @@
     wload[0].wait()
     term(0, 1, gu.at[0])
     send_pair(0, 1)
-    units1 = [(0, 0, "xyz"), (0, 1, "yxz"), (2, 0, "xyz"), (2, 1, "yxz"), (1, 0, "zxy"), (1, 1, "zyx")]
-    units0 = [(1, 0, "zxy"), (1, 1, "zyx"), (0, 0, "xyz"), (2, 0, "yxz"), (0, 1, "zxy"), (2, 1, "yxz")]
+    units1 = [(0, 0, "yxz"), (0, 1, "zxy"), (2, 0, "yxz"), (2, 1, "zyx"), (1, 0, "yxz"), (1, 1, "zyx")]
+    units0 = [(1, 0, "zxy"), (1, 1, "zyx"), (0, 0, "xyz"), (2, 0, "xyz"), (0, 1, "xyz"), (2, 1, "yxz")]
     start1(1, units1)
     start1(0, units0[:2])
     g[...] = g[...] + dot(gu[0], w[0, 1], 1)
@@ -400,27 +405,26 @@
         if ab == 1:
             g[...] = g[...] + dot(rb[0, 0], w[0, 0], 1)
         start1(0, units0[2 + 2 * ab : 4 + 2 * ab])
-    start3(2, units2)
     g[...] = g[...] + dot(rb[0, 1], w[0, 2], 1)
+    result = pltpu.make_async_copy(g, out, go_sem)
     start2(1, units1)
-    start4(2, units2)
-    result = pltpu.make_async_copy(g, out, go_sem)
     result.start()
     start2(0, units0[:4])
+    start3(2, units2)
+    start2(0, units0[4:])
     start3(1, units1)
-    start2(0, units0[4:])
     start3(0, units0[:4])
+    start4(2, units2)
+    start3(0, units0[4:])
+    for groups in order:
+        each_way(groups, "wait_send")
     start4(1, units1)
     finish(2, 0)
     finish(2, 1)
-    start3(0, units0[4:])
-    for groups in order:
-        each_way(groups, "wait_send")
     start4(0, units0)
-    finish(1, 0)
-    finish(1, 1)
-    finish(0, 0)
-    finish(0, 1)
+    for layer in (1, 0):
+        finish(layer, 0)
+        finish(layer, 1)
     result.wait()
 
 
@@ -472,7 +476,7 @@
             vmem(LAYERS, 2, TAPS, 8, 128),
             vmem(LAYERS, 2, TAPS, 8, 128),
             pltpu.SemaphoreType.DMA, dma(CHUNKS, 6), dma(2), dma(LAYERS),
-            dma(LAYERS, 2, CHUNKS), dma(LAYERS, 2, CHUNKS),
+            dma(2, 2, CHUNKS), dma(2, 2, CHUNKS), dma(2, 4, 2), dma(2, 4, 2),
             dma(LAYERS, 3, 2), dma(LAYERS, 3, 2),
             dma(LAYERS, 3, 2), dma(LAYERS, 3, 2), dma(LAYERS, 3, 2),
             dma(LAYERS, 2), dma(LAYERS, 2),

time: 109 us -> 105 us (0.963)
  Pallas kernels: 108 us -> 104 us
    pallas_call x1, Pallas kernels: 105 us -> 101 us  [shards(): pl.pallas_call(kernel, out_shape=(jax.ShapeDtypeStruct((ROWS, C), F32), j...]
where the time goes in v2:
time: 105 us
  Pallas kernels  104 us (99%)
    pallas_call x1, Pallas kernels, shards(): pl.pallas_call(kernel, out_shape=(jax.ShapeDtypeStruct((ROWS, C), F32), j...  101 us
    pallas_call x1, Pallas kernels, shards(): pl.pallas_call(hand_over, out_shape=(jax.ShapeDtypeStruct((ROWS, C), F32)...  2.62 us

profile of v2, /device:TPU:1, one launch (start us, length us, event | category | flops | bytes accessed | tf_op | source)
XLA Modules:
  0.0 104.6 jit_solution(7779944453917929729)
XLA Ops:
  0.6 101.2 %distill.1 = (f32[512,512]{1,0:T(8,128)}, f32[3,3,8,512]{3,2,1,0:T(8,128)}) custom-call(f32[512,512]{1,0:T(8,128)} %feat.1, f32[3,512,512]{2,1,0:T(8,128)} %pre.1, f32[3,512,512]{2,1,0:T(8,128)} %tea.1, f32[512,512]{1,0:T(8,128)} %cot.1, f32[3,3,512,512]{3,2,1,0:T(8,128)} %ker.1), custom_call_target="tpu_custom_call" | custom-call | tf_op jit(solution)/shard_map/distill/pallas_call | solution.py:453
  101.8 2.6 %hand_over.1 = (f32[512,512]{1,0:T(8,128)}, f32[3,3,4,512]{3,2,1,0:T(4,128)}) custom-call(f32[512,512]{1,0:T(8,128)} %get-tuple-element.4.grad, f32[3,3,8,512]{3,2,1,0:T(8,128)} %get-tuple-element.5.blocks), custom_call_target="tpu_custom_call" | custom-call | tf_op jit(solution)/shard_map/hand_over/pallas_call | solution.py:487
